TPU v7x, 32 devices: a whole 2x2x4 slice. The times are simulated.
32 devices in a mesh: rep: 2 (over x), node: 4 (over z), lane: 4 (over y, core).
Axes of the slice: x: 2, y: 2, z: 4, core: 2. Of those that a mesh axis runs over, the one named last changes fastest.
Arguments:
- moe_rows: bfloat16 [64, 7168], P(('rep', 'node', 'lane')), parts along dimension 0, may hold values from -6 to 6
- expert_ids: int32 [64, 8], P(('rep', 'node', 'lane')), parts along dimension 0, may hold values from 0 to 15, all different within a row; in each aligned block of 2 rows (0 to 1, 2 to 3, ...) at most 2 rows name the same one
- route_scores: float32 [64, 8], P(('rep', 'node', 'lane')), parts along dimension 0, may hold values from 0.05 to 1
- gate_proj: bfloat16 [16, 7168, 2048], P('lane', None, 'node'), may hold values from -0.0625 to 0.0625
- up_proj: bfloat16 [16, 7168, 2048], P('lane', None, 'node'), may hold values from -0.0625 to 0.0625
- down_proj: bfloat16 [16, 2048, 7168], P('lane', 'node'), may hold values from -0.125 to 0.125
Outputs:
- moe_out: bfloat16 [64, 7168], P(('rep', 'node', 'lane')), parts along dimension 0
There are 2 independent parts, one for each index of `rep`. A program takes and returns all parts, laid end to end along the dimension named above; an argument that names none is the same for every part. Nothing has to cross between parts.
Inputs may be any that keep to these rules, and one draw needn't show every extreme that they name: `expert_ids`: each row names 8 different experts; the rows of one device name no expert more than 2 times.
All inputs are finite; a program needn't handle non-finite values.
Results may differ from a plain program's by a relative error of at most 0.012.
Values may be sent and summed in bfloat16 or wider, within the bound.
No kernel may reach another device: no remote copies, remote signals or barrier semaphores. Data moves between devices by JAX's collectives and lax.ppermute only.
A program may use at most 128 MiB of HBM per device.

v0:
```python
import jax
import jax.numpy as jnp
from jax import lax
from jax.sharding import PartitionSpec as P

TOP = 8
CAP = 2


route_factor = 2.5


def expert_ffn(slots_in, gate_proj, up_proj, down_proj):
    gate_val = jnp.einsum("kecd,edh->kech", slots_in, gate_proj, preferred_element_type=jnp.float32)
    up_val = jnp.einsum("kecd,edh->kech", slots_in, up_proj, preferred_element_type=jnp.float32)
    hidden = (jax.nn.silu(gate_val) * up_val).astype(jnp.bfloat16)
    return jnp.einsum("kech,ehd->kecd", hidden, down_proj, preferred_element_type=jnp.float32)


def on_device(moe_rows, expert_ids, route_scores, gate_proj, up_proj, down_proj):
    node_count = lax.axis_size("node")
    lane_count = lax.axis_size("lane")
    row_count, model_width = moe_rows.shape
    local_experts = gate_proj.shape[0]
    experts = local_experts * lane_count
    slot_total = experts * CAP
    weights = route_factor * route_scores / jnp.sum(route_scores, axis=1, keepdims=True)
    onehot = (expert_ids[:, :, None] == jnp.arange(experts, dtype=jnp.int32)[None, None, :]).astype(
        jnp.int32
    )
    flat_hits = onehot.reshape((row_count * TOP, experts))
    earlier = jnp.cumsum(flat_hits, axis=0) - flat_hits
    slot_rank = jnp.sum(earlier * flat_hits, axis=1).reshape((row_count, TOP))
    position = expert_ids * CAP + slot_rank
    picked = (
        position[:, :, None] == jnp.arange(slot_total, dtype=jnp.int32)[None, None, :]
    ).astype(jnp.float32)
    dispatch_mat = jnp.max(picked, axis=1).T.astype(jnp.bfloat16)
    combine_mat = jnp.sum(weights[:, :, None] * picked, axis=1)
    send_flat = jnp.dot(dispatch_mat, moe_rows, preferred_element_type=jnp.float32).astype(
        jnp.bfloat16
    )
    send_block = send_flat.reshape((lane_count, local_experts, CAP, model_width))
    copies = jnp.broadcast_to(send_block[None], (node_count,) + send_block.shape)
    copies = copies.reshape((node_count * lane_count, local_experts, CAP, model_width))
    partial_value = expert_ffn(
        lax.all_to_all(copies, ("node", "lane"), split_axis=0, concat_axis=0, tiled=True),
        gate_proj,
        up_proj,
        down_proj,
    )
    returned = lax.all_to_all(
        partial_value.astype(jnp.bfloat16),
        ("node", "lane"),
        split_axis=0,
        concat_axis=0,
        tiled=True,
    )
    returned = returned.astype(jnp.float32).reshape((node_count, experts, CAP, model_width))
    expert_out = jnp.sum(returned, axis=0)
    moe_out = jnp.dot(
        combine_mat,
        expert_out.reshape((slot_total, model_width)),
        precision=lax.Precision.HIGHEST,
        preferred_element_type=jnp.float32,
    )
    return moe_out.astype(jnp.bfloat16)


def solution(mesh):
    in_specs = (
        P(("rep", "node", "lane"), None),
        P(("rep", "node", "lane"), None),
        P(("rep", "node", "lane"), None),
        P("lane", None, "node"),
        P("lane", None, "node"),
        P("lane", "node", None),
    )
    out_specs = P(("rep", "node", "lane"), None)
    return jax.shard_map(
        on_device, mesh=mesh, in_specs=in_specs, out_specs=out_specs, check_vma=False
    )
```

profile of v0, /device:TPU:0, one launch (start us, length us, event | category | flops | bytes accessed | tf_op | source)
XLA Modules:
  0.0 146.1 jit_solution(15134382568448264485)
XLA Ops:
  0.0 0.0 copy-start
  0.0 0.8 eq.29
  0.8 0.8 reduce_sum.37
  1.6 0.7 multiply_divide_fusion
  2.3 0.1 fusion.34
  2.4 0.2 select_reduce_fusion.1
  2.6 0.1 reshape.23
  2.7 0.7 multiply_add_fusion
  3.4 0.1 convert_reduce_fusion.1
  3.5 0.0 copy-done
  3.5 0.3 convolution_convert_fusion
  3.8 0.2 broadcast_in_dim.4
  4.0 1.4 broadcast_in_dim.5
  5.4 49.8 %all_to_all.10 = bf16[16,4,2,7168]{3,2,1,0:T(2,128)(2,1)S(1)} all-to-all(bf16[16,4,2,7168]{3,2,1,0:T(2,128)(2,1)S(1)} %bitcast.47), channel_id=1, replica_groups=mesh['rep'=2,'node'=4,'lane'=4] {'node','lane'}, dimensions={0} | all-to-all | bytes 3670016 | tf_op jit(solution)/shard_map/all_to_all | solution.py:47
  55.2 12.1 %fusion.14 = f32[16,4,2,512]{3,0,2,1:T(8,128)S(1)} fusion(bf16[4,7168,512]{2,1,0:T(8,128)(2,1)} %param.9, bf16[16,4,2,7168]{3,2,1,0:T(2,128)(2,1)S(1)} %all_to_all.10), kind=kOutput, calls=%fused_computation.13 | convolution fusion | flops 939524096 | bytes 31457280 | tf_op jit(solution)/shard_map/kecd,edh->kech/dot_general | solution.py:14
  67.3 12.2 %fusion.29 = bf16[16,4,2,512]{3,0,2,1:T(8,128)(2,1)S(1)} fusion(bf16[4,7168,512]{2,1,0:T(8,128)(2,1)} %param.10, bf16[16,4,2,7168]{3,2,1,0:T(2,128)(2,1)S(1)} %all_to_all.10, f32[16,4,2,512]{3,0,2,1:T(8,128)S(1)} %fusion.14), kind=kOutput, calls=%fused_computation.16 | convolution fusion | flops 939917312 | bytes 31588352 | tf_op jit(solution)/shard_map/kecd,edh->kech/dot_general | solution.py:15
  79.6 14.6 %fusion.9 = bf16[16,4,2,7168]{3,0,2,1:T(8,128)(2,1)S(1)} fusion(bf16[16,4,2,512]{3,0,2,1:T(8,128)(2,1)S(1)} %fusion.29, bf16[4,512,7168]{2,1,0:T(8,128)(2,1)} %param.11), kind=kOutput, calls=%fused_computation.7 | convolution fusion | flops 940441600 | bytes 31326208 | tf_op jit(solution)/shard_map/kech,ehd->kecd/dot_general | solution.py:17
  94.2 1.9 %copy.15 = bf16[16,4,2,7168]{3,2,1,0:T(2,128)(2,1)S(1)} copy(bf16[16,4,2,7168]{3,0,2,1:T(8,128)(2,1)S(1)} %fusion.9) | data formatting | bytes 3670016 | tf_op jit(solution)/shard_map/convert_element_type | solution.py:53
  96.1 46.4 %all_to_all.11 = bf16[16,4,2,7168]{3,2,1,0:T(2,128)(2,1)S(1)} all-to-all(bf16[16,4,2,7168]{3,2,1,0:T(2,128)(2,1)S(1)} %copy.15), channel_id=1, replica_groups=mesh['rep'=2,'node'=4,'lane'=4] {'node','lane'}, dimensions={0} | all-to-all | bytes 3670016 | tf_op jit(solution)/shard_map/all_to_all | solution.py:52
  142.6 0.0 copy-start.1
  142.6 1.7 %convert_reduce_fusion = f32[16,2,7168]{2,1,0:T(2,128)S(1)} fusion(bf16[4,16,2,7168]{3,2,1,0:T(2,128)(2,1)S(1)} %bitcast.48), kind=kLoop, calls=%fused_computation.10 | loop fusion | flops 1605632 | bytes 2752512 | tf_op jit(solution)/shard_map/reduce_sum | solution.py:60
  144.3 0.6 reshape.27
  145.0 1.2 convolution_convert_fusion.1
  146.1 0.0 copy-done.1
  (1 shorter events, 0.0 us)
Async XLA Ops:
  0.0 3.5 %copy-start = (bf16[2,7168]{1,0:T(2,128)(2,1)S(1)}, bf16[2,7168]{1,0:T(2,128)(2,1)}, u32[]{:S(2)}) copy-start(bf16[2,7168]{1,0:T(2,128)(2,1)} %param.6) | copy-start | bytes 86020
  142.6 3.6 %copy-start.1 = (bf16[2,7168]{1,0:T(2,128)(2,1)S(1)}, bf16[2,7168]{1,0:T(2,128)(2,1)}, u32[]{:S(2)}) copy-start(bf16[2,7168]{1,0:T(2,128)(2,1)} %param.6) | copy-start | bytes 86020
where the time goes:
time: 147 us; the launch traced here: 146 us
  blocking collectives  96.2 us (65%)
  matrix products  40.5 us (28%)
  local copies, waits for them, and re-layouts  4.97 us (3%)
  other arithmetic  4.36 us (3%)
    all_to_all x1, blocking collectives, on_device(): lax.all_to_all(copies, ('node', 'lane'), split_axis=0, concat_axis=0, til...  49.8 us
    all_to_all x1, blocking collectives, on_device(): lax.all_to_all(partial_value.astype(jnp.bfloat16), ('node', 'lane'), spli...  46.4 us
    dot_general x1, matrix products, expert_ffn(): jnp.einsum('kech,ehd->kecd', hidden, down_proj, preferred_element_type=jn...  14.6 us
    dot_general x1, matrix products, expert_ffn(): jnp.einsum('kecd,edh->kech', slots_in, up_proj, preferred_element_type=jn...  12.2 us
    dot_general x1, matrix products, expert_ffn(): jnp.einsum('kecd,edh->kech', slots_in, gate_proj, preferred_element_type=...  12.1 us

commit v1 on v0

v1 whole, which is shorter than its diff:
```python
import functools

import jax
import jax.numpy as jnp
from jax import lax
from jax.experimental import pallas as pl
from jax.experimental.pallas import tpu as pltpu
from jax.sharding import PartitionSpec as P

route_factor = 2.5
LANES = 128
ROWS_MXU = 128


def swap(x, axis, bit):
    size = lax.axis_size(axis)
    return lax.ppermute(x, axis, [(i, i ^ bit) for i in range(size)])


def bits_of(size):
    bits, bit = [], size // 2
    while bit:
        bits.append(bit)
        bit //= 2
    return bits


def pack_kernel(experts, rows_ref, ids_ref, scores_ref, out_ref):
    width = rows_ref.shape[1]
    scores = scores_ref[...]
    ids = ids_ref[...]
    weights = route_factor * scores / jnp.sum(scores, axis=1, keepdims=True)
    high = weights.astype(jnp.bfloat16).astype(jnp.float32)
    low = weights - high
    lane = lax.broadcasted_iota(jnp.int32, (ids.shape[0], out_ref.shape[1] - width), 1)
    tail = jnp.zeros(lane.shape, jnp.float32)
    for k in range(ids.shape[1]):
        name = ids[:, k : k + 1]
        tail = tail + jnp.where(lane == name, high[:, k : k + 1], 0.0)
        tail = tail + jnp.where(lane == name + experts, low[:, k : k + 1], 0.0)
    out_ref[:, :width] = rows_ref[...]
    out_ref[:, width:] = tail.astype(jnp.bfloat16)


def pack(rows, ids, scores, experts):
    tail = -(-2 * experts // LANES) * LANES
    return pl.pallas_call(
        functools.partial(pack_kernel, experts),
        out_shape=jax.ShapeDtypeStruct((rows.shape[0], rows.shape[1] + tail), rows.dtype),
        in_specs=[pl.BlockSpec(memory_space=pltpu.VMEM)] * 3,
        out_specs=pl.BlockSpec(memory_space=pltpu.VMEM),
        compiler_params=pltpu.CompilerParams(vmem_limit_bytes=2 << 20),
        name="pack",
    )(rows, ids, scores)


def ffn_kernel(plan, first_ref, *refs):
    experts_here, width, hidden, held, kc, n1, n2, nc, experts = plan
    held_refs, refs = refs[:held], refs[held:]
    (xa_ref, xb_ref, gate_hbm, up_hbm, down_hbm, keep_ref, send_ref, x_buf, tail_buf, h_buf, ring1, ring2, sem1, sem2) = refs
    half = xa_ref.shape[0]
    rows = 2 * half
    ksteps = width // kc
    mats = [(e, m) for e in range(experts_here) for m in range(2)]
    stream = [(e, m, k) for (e, m) in mats[held:] for k in range(ksteps)]
    blocks = width // nc

    def copy1(i):
        e, m, k = stream[i]
        source = (gate_hbm, up_hbm)[m]
        return pltpu.make_async_copy(
            source.at[e, pl.ds(k * kc, kc), :], ring1.at[i % n1], sem1.at[i % n1]
        )

    def copy2(c):
        return pltpu.make_async_copy(
            down_hbm.at[:, :, pl.ds(c * nc, nc)], ring2.at[c % n2], sem2.at[c % n2]
        )

    for i in range(min(n1, len(stream))):
        copy1(i).start()
    for c in range(min(n2, blocks)):
        copy2(c).start()

    x_buf[...] = jnp.zeros_like(x_buf)
    x_buf[:half, :] = xa_ref[:, :width]
    x_buf[half:rows, :] = xb_ref[:, :width]
    tail_buf[:half, :] = xa_ref[:, width:].astype(jnp.float32)
    tail_buf[half:, :] = xb_ref[:, width:].astype(jnp.float32)
    h_buf[...] = jnp.zeros_like(h_buf)
    lane = lax.broadcasted_iota(jnp.int32, tail_buf.shape, 1)

    at = 0
    value = [None, None]
    for index, (e, m) in enumerate(mats):
        if index < held:
            total = jnp.dot(x_buf[...], held_refs[index][0], preferred_element_type=jnp.float32)[:rows]
        else:
            total = jnp.zeros((rows, hidden), jnp.float32)
            for k in range(ksteps):
                copy1(at).wait()
                total = total + jnp.dot(
                    x_buf[:, k * kc : (k + 1) * kc],
                    ring1[at % n1],
                    preferred_element_type=jnp.float32,
                )[:rows]
                if at + n1 < len(stream):
                    copy1(at + n1).start()
                at += 1
        value[m] = total
        if m == 1:
            name = first_ref[0] + e
            mine = jnp.where((lane == name) | (lane == name + experts), tail_buf[...], 0.0)
            weight = jnp.sum(mine, axis=1, keepdims=True)
            gate_val, up_val = value
            h = gate_val / (1.0 + jnp.exp(-gate_val)) * up_val * weight
            h_buf[:rows, e * hidden : (e + 1) * hidden] = h.astype(jnp.bfloat16)

    for c in range(blocks):
        copy2(c).wait()
        total = jnp.dot(
            h_buf[...],
            ring2[c % n2].reshape(experts_here * hidden, nc),
            preferred_element_type=jnp.float32,
        )[:rows].astype(jnp.bfloat16)
        keep_ref[:, c * nc : (c + 1) * nc] = total[:half]
        send_ref[:, c * nc : (c + 1) * nc] = total[half:]
        if c + n2 < blocks:
            copy2(c + n2).start()


def ffn(xa, xb, gate_proj, up_proj, down_proj, first, experts, held=0, kc=1792, n1=6, n2=4, nc=512):
    experts_here, width, hidden = gate_proj.shape
    held = min(held, 2 * experts_here)
    half = xa.shape[0]
    ready = [
        pltpu.with_memory_space_constraint(lax.slice_in_dim((gate_proj, up_proj)[i % 2], i // 2, i // 2 + 1), pltpu.VMEM)
        for i in range(held)
    ]
    any_spec = pl.BlockSpec(memory_space=pl.ANY)
    vmem_spec = pl.BlockSpec(memory_space=pltpu.VMEM)
    rows_mxu = max(ROWS_MXU, -(-2 * half // 16) * 16)
    out = jax.ShapeDtypeStruct((half, width), jnp.bfloat16)
    bytes_all = 3 * gate_proj.size * 2
    return pl.pallas_call(
        functools.partial(ffn_kernel, (experts_here, width, hidden, held, kc, n1, n2, nc, experts)),
        out_shape=(out, out),
        in_specs=[pl.BlockSpec(memory_space=pltpu.SMEM)] + [vmem_spec] * held + [vmem_spec] * 2 + [any_spec] * 3,
        out_specs=(vmem_spec, vmem_spec),
        scratch_shapes=[
            pltpu.VMEM((rows_mxu, width), jnp.bfloat16),
            pltpu.VMEM((2 * half, xa.shape[1] - width), jnp.float32),
            pltpu.VMEM((rows_mxu, experts_here * hidden), jnp.bfloat16),
            pltpu.VMEM((n1, kc, hidden), jnp.bfloat16),
            pltpu.VMEM((n2, experts_here, hidden, nc), jnp.bfloat16),
            pltpu.SemaphoreType.DMA((n1,)),
            pltpu.SemaphoreType.DMA((n2,)),
        ],
        compiler_params=pltpu.CompilerParams(vmem_limit_bytes=27 << 20),
        cost_estimate=pl.CostEstimate(flops=2 * half * bytes_all, bytes_accessed=bytes_all, transcendentals=0),
        name="ffn",
    )(first, *ready, xa, xb, gate_proj, up_proj, down_proj)


def on_device(moe_rows, expert_ids, route_scores, gate_proj, up_proj, down_proj):
    lanes = lax.axis_size("lane")
    experts_here = gate_proj.shape[0]
    experts = experts_here * lanes
    steps = [("node", b) for b in bits_of(lax.axis_size("node"))] + [("lane", b) for b in bits_of(lanes)]
    mine = pack(moe_rows, expert_ids, route_scores, experts)
    for axis, bit in steps[:-1]:
        mine = jnp.concatenate([mine, swap(mine, axis, bit)])
    other = swap(mine, *steps[-1])
    first = (lax.axis_index("lane") * experts_here).astype(jnp.int32).reshape((1,))
    keep, send = ffn(mine, other, gate_proj, up_proj, down_proj, first, experts)
    keep = keep + swap(send, *steps[-1])
    for axis, bit in reversed(steps[:-1]):
        half = keep.shape[0] // 2
        keep = keep[:half] + swap(keep[half:], axis, bit)
    return keep


def solution(mesh):
    in_specs = (
        P(("rep", "node", "lane"), None),
        P(("rep", "node", "lane"), None),
        P(("rep", "node", "lane"), None),
        P("lane", None, "node"),
        P("lane", None, "node"),
        P("lane", "node", None),
    )
    out_specs = P(("rep", "node", "lane"), None)
    return jax.shard_map(
        on_device, mesh=mesh, in_specs=in_specs, out_specs=out_specs, check_vma=False
    )
```

time: 147 us -> 65.7 us (0.45)
  blocking collectives: 96.2 us -> 0 us
  matrix products: 40.5 us -> 0 us
  Pallas kernels: 0 us -> 29.3 us
  waiting for transfers between devices: 0 us -> 18.9 us
  starting transfers between devices: 0 us -> 14 us
  other arithmetic: 4.36 us -> 1.06 us
  local copies, waits for them, and re-layouts: 4.97 us -> 2.18 us
    all_to_all x2 -> x0, blocking collectives: 96.2 us -> none  [the longest x1 49.8 us: on_device(): lax.all_to_all(copies, ('node', 'lane'), split_axis=0, concat_axis=0, til...]
    dot_general x5 -> x0, matrix products: 40.5 us -> none  [the longest x1 14.6 us: expert_ffn(): jnp.einsum('kech,ehd->kecd', hidden, down_proj, preferred_element_type=jn...]
    pallas_call x0 -> x2, Pallas kernels: none -> 29.3 us  [the longest x1 29.1 us: ffn(): pl.pallas_call(functools.partial(ffn_kernel, (experts_here, width, hidden...]
    ppermute x0 -> x8, waiting for transfers between devices: none -> 18.9 us  [swap(): return lax.ppermute(x, axis, [(i, i ^ bit) for i in range(size)])]
    ppermute x0 -> x8, starting transfers between devices: none -> 14 us  [swap(): return lax.ppermute(x, axis, [(i, i ^ bit) for i in range(size)])]
    reduce_sum x3 -> x0, other arithmetic: 2.72 us -> none  [the longest x1 1.74 us: on_device(): expert_out = jnp.sum(returned, axis=0)]
    unnamed x4 -> x6, local copies, waits for them, and re-layouts: 0.01 us -> 2.1 us
    convert_element_type x1 -> x0, local copies, waits for them, and re-layouts: 1.89 us -> none  [on_device(): partial_value.astype(jnp.bfloat16)]
  transfers between devices with their start and end apart: 0 -> 8, of which waited for: 0 -> 8; matrix products, arithmetic and copies ran while one was open for 0% -> 0% of each run, Pallas kernels for 0% -> 0%
where the time goes in v1:
time: 65.7 us; the launch traced here: 65.5 us
  Pallas kernels  29.3 us (45%)
  waiting for transfers between devices  18.9 us (29%)
  starting transfers between devices  14 us (21%)
  local copies, waits for them, and re-layouts  2.18 us (3%)
  other arithmetic  1.06 us (2%)
    pallas_call x1, Pallas kernels, ffn(): pl.pallas_call(functools.partial(ffn_kernel, (experts_here, width, hidden...  29.1 us
    ppermute x8, waiting for transfers between devices, swap(): return lax.ppermute(x, axis, [(i, i ^ bit) for i in range(size)])  18.9 us
    ppermute x8, starting transfers between devices, swap(): return lax.ppermute(x, axis, [(i, i ^ bit) for i in range(size)])  14 us
    unnamed x6, local copies, waits for them, and re-layouts  2.1 us
  transfers between devices with their start and end apart: 8, of which 8 were waited for; matrix products, arithmetic and copies ran while one was open for 0% of the time, Pallas kernels for 0%

profile of v1, /device:TPU:0, one launch (start us, length us, event | category | flops | bytes accessed | tf_op | source)
XLA Modules:
  0.0 65.5 jit_solution(7980895240604036791)
XLA Ops:
  0.0 0.0 copy-start
  0.0 0.7 %copy-done = bf16[2,7168]{1,0:T(2,128)(2,1)S(1)} copy-done((bf16[2,7168]{1,0:T(2,128)(2,1)S(1)}, bf16[2,7168]{1,0:T(2,128)(2,1)}, u32[]{:S(2)}) %copy-start) | copy-done | bytes 28696
  0.7 0.0 copy-start.1
  0.8 0.7 %copy-done.1 = s32[2,8]{1,0:T(2,128)S(1)} copy-done((s32[2,8]{1,0:T(2,128)S(1)}, s32[2,8]{1,0:T(2,128)}, u32[]{:S(2)}) %copy-start.1) | copy-done | bytes 88
  1.4 0.0 copy-start.2
  1.4 0.7 %copy-done.2 = f32[2,8]{1,0:T(2,128)S(1)} copy-done((f32[2,8]{1,0:T(2,128)S(1)}, f32[2,8]{1,0:T(2,128)}, u32[]{:S(2)}) %copy-start.2) | copy-done | bytes 88
  2.1 0.2 pack.1
  2.3 4.1 %collective-permute-start = (bf16[2,7296]{1,0:T(2,128)(2,1)S(1)}, bf16[2,7296]{1,0:T(2,128)(2,1)S(1)}, u32[]{:S(2)}, u32[]{:S(2)}) collective-permute-start(bf16[2,7296]{1,0:T(2,128)(2,1)S(1)} %pack.1), channel_id=1, source_target_pairs={{0,8},{4,12},{8,0},{12,4},{1,9},{5,13},{9,1},{13,5},{2,10},{6,14},... | collective-permute-start | bytes 87560 | tf_op jit(solution)/shard_map/ppermute | solution.py:17
  6.4 2.2 %collective-permute-done = bf16[2,7296]{1,0:T(2,128)(2,1)S(1)} collective-permute-done((bf16[2,7296]{1,0:T(2,128)(2,1)S(1)}, bf16[2,7296]{1,0:T(2,128)(2,1)S(1)}, u32[]{:S(2)}, u32[]{:S(2)}) %collective-permute-start) | collective-permute-done | bytes 29216 | tf_op jit(solution)/shard_map/ppermute | solution.py:17
  8.6 0.1 pad_maximum_fusion.2
  8.7 1.7 %collective-permute-start.1 = (bf16[4,7296]{1,0:T(4,128)(2,1)S(1)}, bf16[4,7296]{1,0:T(4,128)(2,1)S(1)}, u32[]{:S(2)}, u32[]{:S(2)}) collective-permute-start(bf16[4,7296]{1,0:T(4,128)(2,1)S(1)} %pad_maximum_fusion.2), channel_id=1, source_target_pairs={{0,4},{4,0},{8,12},{12,8},{1,5},{5,1},{9,13},{13,9},{2,6},{6,2},{1... | collective-permute-start | bytes 175112 | tf_op jit(solution)/shard_map/ppermute | solution.py:17
  10.3 2.6 %collective-permute-done.1 = bf16[4,7296]{1,0:T(4,128)(2,1)S(1)} collective-permute-done((bf16[4,7296]{1,0:T(4,128)(2,1)S(1)}, bf16[4,7296]{1,0:T(4,128)(2,1)S(1)}, u32[]{:S(2)}, u32[]{:S(2)}) %collective-permute-start.1) | collective-permute-done | bytes 58400 | tf_op jit(solution)/shard_map/ppermute | solution.py:17
  12.9 0.1 pad_maximum_fusion.1
  13.0 1.8 %collective-permute-start.2 = (bf16[8,7296]{1,0:T(8,128)(2,1)S(1)}, bf16[8,7296]{1,0:T(8,128)(2,1)S(1)}, u32[]{:S(2)}, u32[]{:S(2)}) collective-permute-start(bf16[8,7296]{1,0:T(8,128)(2,1)S(1)} %pad_maximum_fusion.1), channel_id=1, source_target_pairs={{0,2},{1,3},{2,0},{3,1},{4,6},{5,7},{6,4},{7,5},{8,10},{9,11},{10,... | collective-permute-start | bytes 350216 | tf_op jit(solution)/shard_map/ppermute | solution.py:17
  14.8 3.1 %collective-permute-done.2 = bf16[8,7296]{1,0:T(8,128)(2,1)S(1)} collective-permute-done((bf16[8,7296]{1,0:T(8,128)(2,1)S(1)}, bf16[8,7296]{1,0:T(8,128)(2,1)S(1)}, u32[]{:S(2)}, u32[]{:S(2)}) %collective-permute-start.2) | collective-permute-done | bytes 116768 | tf_op jit(solution)/shard_map/ppermute | solution.py:17
  17.9 0.2 pad_maximum_fusion.refs_0_
  18.1 0.1 collective-permute-start.3
  18.2 1.5 %collective-permute-done.3.refs_1_ = bf16[16,7296]{1,0:T(8,128)(2,1)S(1)} collective-permute-done((bf16[16,7296]{1,0:T(8,128)(2,1)S(1)}, bf16[16,7296]{1,0:T(8,128)(2,1)S(1)}, u32[]{:S(2)}, u32[]{:S(2)}) %collective-permute-start.3) | collective-permute-done | bytes 233504 | tf_op jit(solution)/shard_map/ppermute | solution.py:17
  19.6 29.1 %ffn.1 = (bf16[16,7168]{1,0:T(8,128)(2,1)S(1)}, bf16[16,7168]{1,0:T(8,128)(2,1)S(1)}) custom-call(s32[1]{0:T(128)} %bitcast.first_ref, bf16[16,7296]{1,0:T(8,128)(2,1)S(1)} %pad_maximum_fusion.refs_0_, bf16[16,7296]{1,0:T(8,128)(2,1)S(1)} %collective-permute-done.3.refs_1_, bf16[4,7168,512]{2,1,0:T(8,128)(2,1)} %refs_2_.1, bf16[4,7168,512]{2,1,0:T(8,128)(2,1)} %refs_3_.1, ...), custom_call_target="tpu_custom_call" | custom-call | flops 2818572288 | bytes 88080384 | tf_op jit(solution)/shard_map/ffn/pallas_call | solution.py:145
  48.7 0.2 collective-permute-start.4
  48.9 1.4 %collective-permute-done.4 = bf16[16,7168]{1,0:T(8,128)(2,1)S(1)} collective-permute-done((bf16[16,7168]{1,0:T(8,128)(2,1)S(1)}, bf16[16,7168]{1,0:T(8,128)(2,1)S(1)}, u32[]{:S(2)}, u32[]{:S(2)}) %collective-permute-start.4) | collective-permute-done | bytes 229408 | tf_op jit(solution)/shard_map/ppermute | solution.py:17
  50.3 0.1 add.12
  50.4 1.8 %collective-permute-start.5 = (bf16[8,7168]{1,0:T(8,128)(2,1)S(1)}, bf16[8,7168]{1,0:T(8,128)(2,1)S(1)}, u32[]{:S(2)}, u32[]{:S(2)}) collective-permute-start(bf16[8,7168]{1,0:T(8,128)(2,1)S(1)} %slice.25), channel_id=1, source_target_pairs={{0,2},{1,3},{2,0},{3,1},{4,6},{5,7},{6,4},{7,5},{8,10},{9,11},{10,... | collective-permute-start | bytes 344072 | tf_op jit(solution)/shard_map/ppermute | solution.py:17
  52.2 3.5 %collective-permute-done.5 = bf16[8,7168]{1,0:T(8,128)(2,1)S(1)} collective-permute-done((bf16[8,7168]{1,0:T(8,128)(2,1)S(1)}, bf16[8,7168]{1,0:T(8,128)(2,1)S(1)}, u32[]{:S(2)}, u32[]{:S(2)}) %collective-permute-start.5) | collective-permute-done | bytes 114720 | tf_op jit(solution)/shard_map/ppermute | solution.py:17
  55.7 1.7 %collective-permute-start.6 = (bf16[4,7168]{1,0:T(4,128)(2,1)S(1)}, bf16[4,7168]{1,0:T(4,128)(2,1)S(1)}, u32[]{:S(2)}, u32[]{:S(2)}) collective-permute-start(bf16[4,7168]{1,0:T(4,128)(2,1)S(1)} %slice.27), channel_id=1, source_target_pairs={{0,4},{4,0},{8,12},{12,8},{1,5},{5,1},{9,13},{13,9},{2,6},{6,2},{1... | collective-permute-start | bytes 172040 | tf_op jit(solution)/shard_map/ppermute | solution.py:17
  57.3 2.6 %collective-permute-done.6 = bf16[4,7168]{1,0:T(4,128)(2,1)S(1)} collective-permute-done((bf16[4,7168]{1,0:T(4,128)(2,1)S(1)}, bf16[4,7168]{1,0:T(4,128)(2,1)S(1)}, u32[]{:S(2)}, u32[]{:S(2)}) %collective-permute-start.6) | collective-permute-done | bytes 57376 | tf_op jit(solution)/shard_map/ppermute | solution.py:17
  60.0 2.7 %collective-permute-start.7 = (bf16[2,7168]{1,0:T(2,128)(2,1)S(1)}, bf16[2,7168]{1,0:T(2,128)(2,1)S(1)}, u32[]{:S(2)}, u32[]{:S(2)}) collective-permute-start(bf16[2,7168]{1,0:T(2,128)(2,1)S(1)} %slice.29), channel_id=1, source_target_pairs={{0,8},{4,12},{8,0},{12,4},{1,9},{5,13},{9,1},{13,5},{2,10},{6,14},... | collective-permute-start | bytes 86024 | tf_op jit(solution)/shard_map/ppermute | solution.py:17
  62.7 2.1 %collective-permute-done.7 = bf16[2,7168]{1,0:T(2,128)(2,1)S(1)} collective-permute-done((bf16[2,7168]{1,0:T(2,128)(2,1)S(1)}, bf16[2,7168]{1,0:T(2,128)(2,1)S(1)}, u32[]{:S(2)}, u32[]{:S(2)}) %collective-permute-start.7) | collective-permute-done | bytes 28704 | tf_op jit(solution)/shard_map/ppermute | solution.py:17
  64.8 0.6 slice_add_fusion.2
  (5 shorter events, 0.1 us)
Async XLA Ops:
  0.0 0.7 %copy-start = (bf16[2,7168]{1,0:T(2,128)(2,1)S(1)}, bf16[2,7168]{1,0:T(2,128)(2,1)}, u32[]{:S(2)}) copy-start(bf16[2,7168]{1,0:T(2,128)(2,1)} %rows_ref.1) | copy-start | bytes 86020
  0.7 0.7 %copy-start.1 = (s32[2,8]{1,0:T(2,128)S(1)}, s32[2,8]{1,0:T(2,128)}, u32[]{:S(2)}) copy-start(s32[2,8]{1,0:T(2,128)} %ids_ref.1) | copy-start | bytes 196
  1.4 0.7 %copy-start.2 = (f32[2,8]{1,0:T(2,128)S(1)}, f32[2,8]{1,0:T(2,128)}, u32[]{:S(2)}) copy-start(f32[2,8]{1,0:T(2,128)} %scores_ref.1) | copy-start | bytes 196
  2.3 6.3 %collective-permute-start = (bf16[2,7296]{1,0:T(2,128)(2,1)S(1)}, bf16[2,7296]{1,0:T(2,128)(2,1)S(1)}, u32[]{:S(2)}, u32[]{:S(2)}) collective-permute-start(bf16[2,7296]{1,0:T(2,128)(2,1)S(1)} %pack.1), channel_id=1, source_target_pairs={{0,8},{4,12},{8,0},{12,4},{1,9},{5,13},{9,1},{13,5},{2,10},{6,14},... | collective-permute-start | bytes 87560 | tf_op jit(solution)/shard_map/ppermute | solution.py:17
  8.7 4.3 %collective-permute-start.1 = (bf16[4,7296]{1,0:T(4,128)(2,1)S(1)}, bf16[4,7296]{1,0:T(4,128)(2,1)S(1)}, u32[]{:S(2)}, u32[]{:S(2)}) collective-permute-start(bf16[4,7296]{1,0:T(4,128)(2,1)S(1)} %pad_maximum_fusion.2), channel_id=1, source_target_pairs={{0,4},{4,0},{8,12},{12,8},{1,5},{5,1},{9,13},{13,9},{2,6},{6,2},{1... | collective-permute-start | bytes 175112 | tf_op jit(solution)/shard_map/ppermute | solution.py:17
  13.0 4.9 %collective-permute-start.2 = (bf16[8,7296]{1,0:T(8,128)(2,1)S(1)}, bf16[8,7296]{1,0:T(8,128)(2,1)S(1)}, u32[]{:S(2)}, u32[]{:S(2)}) collective-permute-start(bf16[8,7296]{1,0:T(8,128)(2,1)S(1)} %pad_maximum_fusion.1), channel_id=1, source_target_pairs={{0,2},{1,3},{2,0},{3,1},{4,6},{5,7},{6,4},{7,5},{8,10},{9,11},{10,... | collective-permute-start | bytes 350216 | tf_op jit(solution)/shard_map/ppermute | solution.py:17
  18.1 1.6 %collective-permute-start.3 = (bf16[16,7296]{1,0:T(8,128)(2,1)S(1)}, bf16[16,7296]{1,0:T(8,128)(2,1)S(1)}, u32[]{:S(2)}, u32[]{:S(2)}) collective-permute-start(bf16[16,7296]{1,0:T(8,128)(2,1)S(1)} %pad_maximum_fusion.refs_0_), channel_id=1, source_target_pairs={{0,1},{1,0},{2,3},{3,2},{4,5},{5,4},{6,7},{7,6},{8,9},{9,8},{10,11... | collective-permute-start | bytes 700424 | tf_op jit(solution)/shard_map/ppermute | solution.py:17
  48.7 1.6 %collective-permute-start.4 = (bf16[16,7168]{1,0:T(8,128)(2,1)S(1)}, bf16[16,7168]{1,0:T(8,128)(2,1)S(1)}, u32[]{:S(2)}, u32[]{:S(2)}) collective-permute-start(bf16[16,7168]{1,0:T(8,128)(2,1)S(1)} %get-tuple-element.8), channel_id=1, source_target_pairs={{0,1},{1,0},{2,3},{3,2},{4,5},{5,4},{6,7},{7,6},{8,9},{9,8},{10,11... | collective-permute-start | bytes 688136 | tf_op jit(solution)/shard_map/ppermute | solution.py:17
  50.4 5.3 %collective-permute-start.5 = (bf16[8,7168]{1,0:T(8,128)(2,1)S(1)}, bf16[8,7168]{1,0:T(8,128)(2,1)S(1)}, u32[]{:S(2)}, u32[]{:S(2)}) collective-permute-start(bf16[8,7168]{1,0:T(8,128)(2,1)S(1)} %slice.25), channel_id=1, source_target_pairs={{0,2},{1,3},{2,0},{3,1},{4,6},{5,7},{6,4},{7,5},{8,10},{9,11},{10,... | collective-permute-start | bytes 344072 | tf_op jit(solution)/shard_map/ppermute | solution.py:17
  55.7 4.2 %collective-permute-start.6 = (bf16[4,7168]{1,0:T(4,128)(2,1)S(1)}, bf16[4,7168]{1,0:T(4,128)(2,1)S(1)}, u32[]{:S(2)}, u32[]{:S(2)}) collective-permute-start(bf16[4,7168]{1,0:T(4,128)(2,1)S(1)} %slice.27), channel_id=1, source_target_pairs={{0,4},{4,0},{8,12},{12,8},{1,5},{5,1},{9,13},{13,9},{2,6},{6,2},{1... | collective-permute-start | bytes 172040 | tf_op jit(solution)/shard_map/ppermute | solution.py:17
  60.0 4.8 %collective-permute-start.7 = (bf16[2,7168]{1,0:T(2,128)(2,1)S(1)}, bf16[2,7168]{1,0:T(2,128)(2,1)S(1)}, u32[]{:S(2)}, u32[]{:S(2)}) collective-permute-start(bf16[2,7168]{1,0:T(2,128)(2,1)S(1)} %slice.29), channel_id=1, source_target_pairs={{0,8},{4,12},{8,0},{12,4},{1,9},{5,13},{9,1},{13,5},{2,10},{6,14},... | collective-permute-start | bytes 86024 | tf_op jit(solution)/shard_map/ppermute | solution.py:17
